TPU v7x, 128 devices: a whole 4x4x4 slice. The times are simulated.
128 devices in a mesh: ray: 16 (over x, z), tile: 8 (over y, core).
Axes of the slice: x: 4, y: 4, z: 4, core: 2. Of those that a mesh axis runs over, the one named last changes fastest.
Arguments:
- data: float32 [64, 262144], P(None, ('ray', 'tile')), may hold values from -6 to 6
- sensitivity: bfloat16 [4096, 256, 512], P(('ray', 'tile')), may hold values from -0.25 to 0.25
- block_tiles: int32 [128, 8, 4], P(('ray', 'tile')), may hold values from 0 to 47
- block_bundles: int32 [128, 8, 4], P(('ray', 'tile')), may hold values from 0 to 7
Outputs:
- solution: float32 [64, 196608], P(None, 'tile')
- residual: float32 [64, 262144], P(None, ('ray', 'tile'))
Inputs may be any that keep to these rules, and one draw needn't show every extreme that they name: `block_tiles`: position of the block's tile among the 48 tiles of the owner given by the second index. `block_bundles`: the block's ray bundle among the device's 8 bundles.
All inputs are finite; a program needn't handle non-finite values.
Results may differ from a plain program's by a relative error of at most 0.004.
The roundings to bfloat16 on the way count: a program that leaves them out, or rounds other values in their place, can miss the bound.
Values may be sent and summed in bfloat16 or wider, within the bound.
A program may use at most 128 MiB of HBM per device.

v0:
```python
import jax
import jax.numpy as jnp
from jax import lax
from jax.sharding import PartitionSpec as P

RB = 256
CB = 512
ITERS = 2
BUND_DEV = 8
TILE_DEV = 48
eps_norm = 1e-06


def per_device(data, sensitivity, block_tiles, block_bundles):
    columns = data.shape[0]
    bundles = block_bundles.reshape(-1)
    requests = lax.all_to_all(block_tiles, "tile", split_axis=1, concat_axis=1, tiled=True).reshape(
        -1
    )
    bundle_onehot = (bundles[:, None] == jnp.arange(BUND_DEV, dtype=jnp.int32)[None, :]).astype(
        jnp.float32
    )
    owner_onehot = (requests[:, None] == jnp.arange(TILE_DEV, dtype=jnp.int32)[None, :]).astype(
        jnp.bfloat16
    )

    def fetch(field_bf):
        owned = field_bf.reshape(columns, TILE_DEV, CB)
        outgoing = jnp.take(owned, requests, axis=1)
        tiles = lax.all_to_all(outgoing, "tile", split_axis=1, concat_axis=1, tiled=True)
        return tiles

    def forward(field_bf):
        tiles = fetch(field_bf)
        partial_value = jnp.einsum(
            "cnk,nrk->ncr", tiles, sensitivity, preferred_element_type=jnp.float32
        )
        summed = jnp.einsum(
            "ncr,nb->cbr", partial_value, bundle_onehot, precision=lax.Precision.HIGHEST
        )
        return summed.reshape(columns, BUND_DEV * RB)

    def adjoint(rays_bf):
        picked = jnp.take(rays_bf.reshape(columns, BUND_DEV, RB), bundles, axis=1)
        terms = jnp.einsum(
            "cnr,nrk->cnk", picked, sensitivity, preferred_element_type=jnp.float32
        ).astype(jnp.bfloat16)
        arrived = lax.all_to_all(terms, "tile", split_axis=1, concat_axis=1, tiled=True)
        owned = jnp.einsum(
            "cnk,nt->ctk", arrived, owner_onehot, preferred_element_type=jnp.float32
        ).reshape(columns, TILE_DEV * CB)
        total = lax.psum(owned, "ray")
        return total

    def cell_norm(field):
        local = jnp.sum(field * field, axis=1)
        total = lax.psum(local, "tile")
        return jnp.sqrt(total + eps_norm)

    def ray_norm(rays):
        total = lax.psum(jnp.sum(rays * rays, axis=1), ("ray", "tile"))
        return jnp.sqrt(total + eps_norm)

    beta_now = ray_norm(data)
    rays_dir = data / beta_now[:, None]
    model_dir = adjoint(rays_dir.astype(jnp.bfloat16))
    alpha_now = cell_norm(model_dir)
    model_dir = model_dir / alpha_now[:, None]
    search = model_dir
    solution = jnp.zeros_like(model_dir)
    phi_bar = beta_now
    rho_bar = alpha_now
    for step in range(ITERS):
        rounded = model_dir.astype(jnp.bfloat16)
        rays_dir = forward(rounded) - alpha_now[:, None] * rays_dir
        beta_now = ray_norm(rays_dir)
        rays_dir = rays_dir / beta_now[:, None]
        rho_now = jnp.sqrt(rho_bar * rho_bar + beta_now * beta_now)
        cosine = rho_bar / rho_now
        sine_part = beta_now / rho_now
        phi_now = cosine * phi_bar
        phi_bar = sine_part * phi_bar
        solution = solution + (phi_now / rho_now)[:, None] * search
        if step + 1 < ITERS:
            model_dir = adjoint(rays_dir.astype(jnp.bfloat16)) - beta_now[:, None] * model_dir
            alpha_now = cell_norm(model_dir)
            model_dir = model_dir / alpha_now[:, None]
            theta_now = sine_part * alpha_now
            rho_bar = -cosine * alpha_now
            search = model_dir - (theta_now / rho_now)[:, None] * search
    residual = data - forward(solution.astype(jnp.bfloat16))
    return (solution, residual)


def solution(mesh):
    return jax.shard_map(
        per_device,
        mesh=mesh,
        in_specs=(
            P(None, ("ray", "tile")),
            P(("ray", "tile"), None, None),
            P(("ray", "tile"), None, None),
            P(("ray", "tile"), None, None),
        ),
        out_specs=(P(None, "tile"), P(None, ("ray", "tile"))),
        check_vma=False,
    )
```

profile of v0, /device:TPU:1, one launch (start us, length us, event | category | flops | bytes accessed | tf_op | source)
XLA Modules:
  0.0 731.6 jit_solution(17410393598439722855)
XLA Ops:
  8.5 6.0 all-to-all-start
  16.5 67.7 %psum.49 = f32[64]{0:T(128)S(1)} all-reduce(f32[64]{0:T(128)S(1)} %multiply_reduce_fusion.4), channel_id=1, replica_groups=mesh['ray'=16,'tile'=8] {'ray','tile'}, use_global_device_ids=true, to_apply=%region_1.0 | all-reduce | flops 64 | bytes 512 | tf_op jit(solution)/shard_map/psum | solution.py:61
  86.1 6.3 convert_bitcast_fusion.1
  92.4 4.4 all-to-all-start.1
  98.1 25.1 %all-to-all-done.1 = bf16[64,32,512]{2,0,1:T(8,128)(2,1)S(1)} async-done(((bf16[64,32,512]{2,0,1:T(8,128)(2,1)}), bf16[64,32,512]{2,0,1:T(8,128)(2,1)S(1)}, u32[]{:S(2)}, u32[]{:S(2)}) %all-to-all-start.1) | async-done | bytes 2097184 | tf_op jit(solution)/shard_map/all_to_all | solution.py:48
  124.9 6.3 copy.39
  131.3 119.1 %all-reduce.3.cloned.1.call-done = f32[64,24576]{1,0:T(8,128)} async-done(((f32[64,24576]{1,0:T(8,128)}), f32[64,24576]{1,0:T(8,128)}) %all-reduce.3.cloned.1.call-update) | async-done | bytes 6291472 | tf_op jit(solution)/shard_map/psum | solution.py:52
  253.7 12.4 %psum.51 = f32[64]{0:T(128)S(1)} all-reduce(f32[64]{0:T(128)S(1)} %multiply_reduce_fusion.1), channel_id=1, replica_groups=mesh['ray'=16,'tile'=8] {'tile'}, use_global_device_ids=true, to_apply=%region_4.6 | all-reduce | flops 64 | bytes 512 | tf_op jit(solution)/shard_map/psum | solution.py:57
  273.7 31.7 %all_to_all.30 = bf16[64,32,512]{2,0,1:T(8,128)(2,1)S(1)} all-to-all(bf16[64,32,512]{2,0,1:T(8,128)(2,1)S(1)} %select_bitcast_fusion.2), channel_id=1, replica_groups=mesh['ray'=16,'tile'=8] {'tile'}, dimensions={1} | all-to-all | bytes 4194304 | tf_op jit(solution)/shard_map/all_to_all | solution.py:30
  305.4 6.0 fusion.41
  313.9 64.5 %psum.52 = f32[64]{0:T(128)S(1)} all-reduce(f32[64]{0:T(128)S(1)} %get-tuple-element.11), channel_id=1, replica_groups=mesh['ray'=16,'tile'=8] {'ray','tile'}, use_global_device_ids=true, to_apply=%region_6.0 | all-reduce | flops 64 | bytes 512 | tf_op jit(solution)/shard_map/psum | solution.py:61
  379.2 5.0 convert_bitcast_fusion
  384.2 30.1 %all_to_all.31 = bf16[64,32,512]{2,0,1:T(8,128)(2,1)S(1)} all-to-all(bf16[64,32,512]{2,0,1:T(8,128)(2,1)S(1)} %convert_bitcast_fusion), channel_id=1, replica_groups=mesh['ray'=16,'tile'=8] {'tile'}, dimensions={1} | all-to-all | bytes 4194304 | tf_op jit(solution)/shard_map/all_to_all | solution.py:48
  416.0 6.3 copy.41
  422.3 118.9 %all-reduce.5.cloned.1.call-done = f32[64,24576]{1,0:T(8,128)} async-done(((f32[64,24576]{1,0:T(8,128)}), f32[64,24576]{1,0:T(8,128)}) %all-reduce.5.cloned.1.call-update) | async-done | bytes 6291472 | tf_op jit(solution)/shard_map/psum | solution.py:52
  541.2 5.8 multiply_reduce_fusion
  547.0 12.4 %psum.54 = f32[64]{0:T(128)S(1)} all-reduce(f32[64]{0:T(128)S(1)} %multiply_reduce_fusion), channel_id=1, replica_groups=mesh['ray'=16,'tile'=8] {'tile'}, use_global_device_ids=true, to_apply=%region_9.12 | all-reduce | flops 64 | bytes 512 | tf_op jit(solution)/shard_map/psum | solution.py:57
  559.4 5.2 fusion.10
  568.9 31.7 %all_to_all.32 = bf16[64,32,512]{2,0,1:T(8,128)(2,1)S(1)} all-to-all(bf16[64,32,512]{2,0,1:T(8,128)(2,1)S(1)} %select_bitcast_fusion.1), channel_id=1, replica_groups=mesh['ray'=16,'tile'=8] {'tile'}, dimensions={1} | all-to-all | bytes 4194304 | tf_op jit(solution)/shard_map/all_to_all | solution.py:30
  600.7 6.0 fusion.42
  609.1 64.8 %psum.55 = f32[64]{0:T(128)S(1)} all-reduce(f32[64]{0:T(128)S(1)} %multiply_reduce_fusion.2), channel_id=1, replica_groups=mesh['ray'=16,'tile'=8] {'ray','tile'}, use_global_device_ids=true, to_apply=%region_11.14 | all-reduce | flops 64 | bytes 512 | tf_op jit(solution)/shard_map/psum | solution.py:61
  673.9 7.4 %fusion.38 = (bf16[64,24576]{1,0:T(8,128)(2,1)S(1)}, f32[64,24576]{1,0:T(8,128)}) fusion(f32[64]{0:T(128)S(1)} %multiply_divide_fusion, f32[64]{0:T(128)S(1)} %add_sqrt_fusion, f32[64,24576]{1,0:T(8,128)} %all-reduce.5.cloned.1.call-done, f32[64]{0:T(128)S(1)} %get-tuple-element.13, f32[64]{0:T(128)S(1)} %get-tuple-element.9, ...), kind=kLoop, calls=%fused_computation.76 | loop fusion | flops 15728640 | bytes 22021632 | tf_op jit(solution)/shard_map/convert_element_type | solution.py:91
  685.6 30.1 %all_to_all.33 = bf16[64,32,512]{2,0,1:T(8,128)(2,1)S(1)} all-to-all(bf16[64,32,512]{2,0,1:T(8,128)(2,1)S(1)} %select_bitcast_fusion), channel_id=1, replica_groups=mesh['ray'=16,'tile'=8] {'tile'}, dimensions={1} | all-to-all | bytes 4194304 | tf_op jit(solution)/shard_map/all_to_all | solution.py:30
  715.7 6.0 fusion.43
  (60 shorter events, 37.9 us)
Async XLA Ops:
  8.5 83.9 %all-to-all-start = ((s32[1,8,4]{2,0,1:T(1,128)}), s32[1,8,4]{2,0,1:T(1,128)S(1)}, u32[]{:S(2)}, u32[]{:S(2)}) async-start(s32[1,8,4]{2,0,1:T(1,128)} %copy.22), calls=%async_computation | async-start | bytes 8192 | tf_op jit(solution)/shard_map/all_to_all | solution.py:17
  92.4 30.8 %all-to-all-start.1 = ((bf16[64,32,512]{2,0,1:T(8,128)(2,1)}), bf16[64,32,512]{2,0,1:T(8,128)(2,1)S(1)}, u32[]{:S(2)}, u32[]{:S(2)}) async-start(bf16[64,32,512]{2,0,1:T(8,128)(2,1)} %convert_bitcast_fusion.1), calls=%async_computation.1 | async-start | bytes 4194304 | tf_op jit(solution)/shard_map/all_to_all | solution.py:48
  96.8 153.6 %all-reduce.3.cloned.1.call-start = ((), (), s32[]{:S(2)}) async-start(), calls=%async_computation.6 | async-start | bytes 12582912 | tf_op jit(solution)/shard_map/psum | solution.py:52
  131.2 410.0 %all-reduce.5.cloned.1.call-start = ((), (), s32[]{:S(2)}) async-start(), calls=%async_computation.7 | async-start | bytes 12582912 | tf_op jit(solution)/shard_map/psum | solution.py:52
  311.4 2.1 copy-start
  313.9 64.7 %copy-start.2 = (f32[64,2048]{1,0:T(8,128)}, f32[64,2048]{1,0:T(8,128)S(1)}, u32[]{:S(2)}) copy-start(f32[64,2048]{1,0:T(8,128)S(1)} %get-tuple-element.12) | copy-start | bytes 1572868
  606.7 2.1 copy-start.3
  721.7 2.1 copy-start.1
Sparse Core Ops, SparseCore 0:
  131.3 119.0 all-reduce.2
  422.4 118.6 all-reduce.4
where the time goes:
time: 733 us; the launch traced here: 732 us
  blocking collectives  346 us (47%)
  waiting for transfers between devices  263 us (36%)
  matrix products  38.8 us (5%)
  other arithmetic  35 us (5%)
  local copies, waits for them, and re-layouts  24.4 us (3%)
  between operations  14.3 us (2%)
  starting transfers between devices  10.4 us (1%)
    psum x2, waiting for transfers between devices, adjoint(): total = lax.psum(owned, 'ray')  238 us
    psum x3, blocking collectives, ray_norm(): total = lax.psum(jnp.sum(rays * rays, axis=1), ('ray', 'tile'))  197 us
    all_to_all x3, blocking collectives, fetch(): lax.all_to_all(outgoing, 'tile', split_axis=1, concat_axis=1, tiled=True)  93.6 us
    all_to_all x1, blocking collectives, adjoint(): lax.all_to_all(terms, 'tile', split_axis=1, concat_axis=1, tiled=True)  30.1 us
    all_to_all x1, waiting for transfers between devices, adjoint(): lax.all_to_all(terms, 'tile', split_axis=1, concat_axis=1, tiled=True)  25.1 us
    psum x2, blocking collectives, cell_norm(): total = lax.psum(local, 'tile')  24.9 us
    dot_general x3, matrix products, forward(): jnp.einsum('cnk,nrk->ncr', tiles, sensitivity, preferred_element_type=jnp...  18.1 us
    unnamed x15, local copies, waits for them, and re-layouts  15.1 us
  transfers between devices with their start and end apart: 4, of which 3 were waited for; matrix products, arithmetic and copies ran while one was open for 2% of the time, Pallas kernels for 0%

commit v1 on v0

--- a/solution.py
+++ b/solution.py
@@ -58,7 +58,7 @@
         return jnp.sqrt(total + eps_norm)
 
     def ray_norm(rays):
-        total = lax.psum(jnp.sum(rays * rays, axis=1), ("ray", "tile"))
+        total = lax.psum(lax.psum(jnp.sum(rays * rays, axis=1), "tile"), "ray")
         return jnp.sqrt(total + eps_norm)
 
     beta_now = ray_norm(data)

time: 733 us -> 690 us (0.941)
  blocking collectives: 346 us -> 297 us
  starting transfers between devices: 10.4 us -> 19.9 us
    psum x3 -> x6, blocking collectives: 197 us -> 134 us  [ray_norm(): total = lax.psum(lax.psum(jnp.sum(rays * rays, axis=1), 'tile'), 'ray')]
    all_to_all x1, starting transfers between devices: 4.4 us -> 13.9 us  [adjoint(): lax.all_to_all(terms, 'tile', split_axis=1, concat_axis=1, tiled=True)]
where the time goes in v1:
time: 690 us; the launch traced here: 689 us
  blocking collectives  297 us (43%)
  waiting for transfers between devices  260 us (38%)
  matrix products  38.8 us (6%)
  other arithmetic  35 us (5%)
  local copies, waits for them, and re-layouts  24.3 us (4%)
  starting transfers between devices  19.9 us (3%)
  between operations  14.3 us (2%)
    psum x2, waiting for transfers between devices, adjoint(): total = lax.psum(owned, 'ray')  234 us
    psum x6, blocking collectives, ray_norm(): total = lax.psum(lax.psum(jnp.sum(rays * rays, axis=1), 'tile'), 'ray')  134 us
    all_to_all x3, blocking collectives, fetch(): lax.all_to_all(outgoing, 'tile', split_axis=1, concat_axis=1, tiled=True)  100 us
    all_to_all x1, blocking collectives, adjoint(): lax.all_to_all(terms, 'tile', split_axis=1, concat_axis=1, tiled=True)  37 us
    psum x2, blocking collectives, cell_norm(): total = lax.psum(local, 'tile')  25.1 us
    all_to_all x1, waiting for transfers between devices, adjoint(): lax.all_to_all(terms, 'tile', split_axis=1, concat_axis=1, tiled=True)  25.1 us
    dot_general x3, matrix products, forward(): jnp.einsum('cnk,nrk->ncr', tiles, sensitivity, preferred_element_type=jnp...  18.1 us
    unnamed x15, local copies, waits for them, and re-layouts  15.1 us
  transfers between devices with their start and end apart: 4, of which 3 were waited for; matrix products, arithmetic and copies ran while one was open for 2% of the time, Pallas kernels for 0%

profile of v1, /device:TPU:1, one launch (start us, length us, event | category | flops | bytes accessed | tf_op | source)
XLA Modules:
  0.0 689.0 jit_solution(5747341820461819291)
XLA Ops:
  8.5 6.0 all-to-all-start
  16.5 12.2 %psum.70 = f32[64]{0:T(128)S(1)} all-reduce(f32[64]{0:T(128)S(1)} %multiply_reduce_fusion.4), channel_id=1, replica_groups=mesh['ray'=16,'tile'=8] {'tile'}, use_global_device_ids=true, to_apply=%region_1.0 | all-reduce | flops 64 | bytes 512 | tf_op jit(solution)/shard_map/psum | solution.py:61
  28.7 34.5 %psum.71 = f32[64]{0:T(128)S(1)} all-reduce(f32[64]{0:T(128)S(1)} %psum.70), channel_id=1, replica_groups=mesh['ray'=16,'tile'=8] {'ray'}, use_global_device_ids=true, to_apply=%region_2.0 | all-reduce | flops 64 | bytes 512 | tf_op jit(solution)/shard_map/psum | solution.py:61
  65.0 6.3 convert_bitcast_fusion.1
  71.3 13.9 %all-to-all-start.1 = ((bf16[64,32,512]{2,0,1:T(8,128)(2,1)}), bf16[64,32,512]{2,0,1:T(8,128)(2,1)S(1)}, u32[]{:S(2)}, u32[]{:S(2)}) async-start(bf16[64,32,512]{2,0,1:T(8,128)(2,1)} %convert_bitcast_fusion.1), calls=%async_computation.1 | async-start | bytes 4194304 | tf_op jit(solution)/shard_map/all_to_all | solution.py:48
  86.5 25.1 %all-to-all-done.1 = bf16[64,32,512]{2,0,1:T(8,128)(2,1)S(1)} async-done(((bf16[64,32,512]{2,0,1:T(8,128)(2,1)}), bf16[64,32,512]{2,0,1:T(8,128)(2,1)S(1)}, u32[]{:S(2)}, u32[]{:S(2)}) %all-to-all-start.1) | async-done | bytes 2097184 | tf_op jit(solution)/shard_map/all_to_all | solution.py:48
  113.3 6.3 copy.39
  119.7 117.1 %all-reduce.3.cloned.1.call-done = f32[64,24576]{1,0:T(8,128)} async-done(((f32[64,24576]{1,0:T(8,128)}), f32[64,24576]{1,0:T(8,128)}) %all-reduce.3.cloned.1.call-update) | async-done | bytes 6291472 | tf_op jit(solution)/shard_map/psum | solution.py:52
  240.1 12.4 %psum.73 = f32[64]{0:T(128)S(1)} all-reduce(f32[64]{0:T(128)S(1)} %multiply_reduce_fusion.1), channel_id=1, replica_groups=mesh['ray'=16,'tile'=8] {'tile'}, use_global_device_ids=true, to_apply=%region_5.7 | all-reduce | flops 64 | bytes 512 | tf_op jit(solution)/shard_map/psum | solution.py:57
  260.1 31.7 %all_to_all.30 = bf16[64,32,512]{2,0,1:T(8,128)(2,1)S(1)} all-to-all(bf16[64,32,512]{2,0,1:T(8,128)(2,1)S(1)} %select_bitcast_fusion.2), channel_id=1, replica_groups=mesh['ray'=16,'tile'=8] {'tile'}, dimensions={1} | all-to-all | bytes 4194304 | tf_op jit(solution)/shard_map/all_to_all | solution.py:30
  291.8 6.0 fusion.41
  300.3 12.8 %psum.74 = f32[64]{0:T(128)S(1)} all-reduce(f32[64]{0:T(128)S(1)} %get-tuple-element.11), channel_id=1, replica_groups=mesh['ray'=16,'tile'=8] {'tile'}, use_global_device_ids=true, to_apply=%region_7.0 | all-reduce | flops 64 | bytes 512 | tf_op jit(solution)/shard_map/psum | solution.py:61
  313.1 31.1 %psum.75 = f32[64]{0:T(128)S(1)} all-reduce(f32[64]{0:T(128)S(1)} %psum.74), channel_id=1, replica_groups=mesh['ray'=16,'tile'=8] {'ray'}, use_global_device_ids=true, to_apply=%region_8.11 | all-reduce | flops 64 | bytes 512 | tf_op jit(solution)/shard_map/psum | solution.py:61
  350.0 37.0 %all_to_all.31 = bf16[64,32,512]{2,0,1:T(8,128)(2,1)S(1)} all-to-all(bf16[64,32,512]{2,0,1:T(8,128)(2,1)S(1)} %convert_bitcast_fusion), channel_id=1, replica_groups=mesh['ray'=16,'tile'=8] {'tile'}, dimensions={1} | all-to-all | bytes 4194304 | tf_op jit(solution)/shard_map/all_to_all | solution.py:48
  388.7 6.3 copy.41
  395.0 117.3 %all-reduce.5.cloned.1.call-done = f32[64,24576]{1,0:T(8,128)} async-done(((f32[64,24576]{1,0:T(8,128)}), f32[64,24576]{1,0:T(8,128)}) %all-reduce.5.cloned.1.call-update) | async-done | bytes 6291472 | tf_op jit(solution)/shard_map/psum | solution.py:52
  518.1 12.7 %psum.77 = f32[64]{0:T(128)S(1)} all-reduce(f32[64]{0:T(128)S(1)} %multiply_reduce_fusion), channel_id=1, replica_groups=mesh['ray'=16,'tile'=8] {'tile'}, use_global_device_ids=true, to_apply=%region_11.14 | all-reduce | flops 64 | bytes 512 | tf_op jit(solution)/shard_map/psum | solution.py:57
  540.3 31.7 %all_to_all.32 = bf16[64,32,512]{2,0,1:T(8,128)(2,1)S(1)} all-to-all(bf16[64,32,512]{2,0,1:T(8,128)(2,1)S(1)} %select_bitcast_fusion.1), channel_id=1, replica_groups=mesh['ray'=16,'tile'=8] {'tile'}, dimensions={1} | all-to-all | bytes 4194304 | tf_op jit(solution)/shard_map/all_to_all | solution.py:30
  572.0 6.0 fusion.42
  580.5 12.8 %psum.78 = f32[64]{0:T(128)S(1)} all-reduce(f32[64]{0:T(128)S(1)} %multiply_reduce_fusion.2), channel_id=1, replica_groups=mesh['ray'=16,'tile'=8] {'tile'}, use_global_device_ids=true, to_apply=%region_13.16 | all-reduce | flops 64 | bytes 512 | tf_op jit(solution)/shard_map/psum | solution.py:61
  593.3 31.1 %psum.79 = f32[64]{0:T(128)S(1)} all-reduce(f32[64]{0:T(128)S(1)} %psum.78), channel_id=1, replica_groups=mesh['ray'=16,'tile'=8] {'ray'}, use_global_device_ids=true, to_apply=%region_14.17 | all-reduce | flops 64 | bytes 512 | tf_op jit(solution)/shard_map/psum | solution.py:61
  624.4 7.4 %fusion.38 = (bf16[64,24576]{1,0:T(8,128)(2,1)S(1)}, f32[64,24576]{1,0:T(8,128)}) fusion(f32[64]{0:T(128)S(1)} %multiply_divide_fusion, f32[64]{0:T(128)S(1)} %add_sqrt_fusion, f32[64,24576]{1,0:T(8,128)} %all-reduce.5.cloned.1.call-done, f32[64]{0:T(128)S(1)} %get-tuple-element.13, f32[64]{0:T(128)S(1)} %get-tuple-element.9, ...), kind=kLoop, calls=%fused_computation.76 | loop fusion | flops 15728640 | bytes 22021632 | tf_op jit(solution)/shard_map/convert_element_type | solution.py:91
  636.1 37.0 %all_to_all.33 = bf16[64,32,512]{2,0,1:T(8,128)(2,1)S(1)} all-to-all(bf16[64,32,512]{2,0,1:T(8,128)(2,1)S(1)} %select_bitcast_fusion), channel_id=1, replica_groups=mesh['ray'=16,'tile'=8] {'tile'}, dimensions={1} | all-to-all | bytes 4194304 | tf_op jit(solution)/shard_map/all_to_all | solution.py:30
  673.0 6.0 fusion.43
  (63 shorter events, 53.9 us)
Async XLA Ops:
  8.5 62.8 %all-to-all-start = ((s32[1,8,4]{2,0,1:T(1,128)}), s32[1,8,4]{2,0,1:T(1,128)S(1)}, u32[]{:S(2)}, u32[]{:S(2)}) async-start(s32[1,8,4]{2,0,1:T(1,128)} %copy.22), calls=%async_computation | async-start | bytes 8192 | tf_op jit(solution)/shard_map/all_to_all | solution.py:17
  71.3 40.3 %all-to-all-start.1 = ((bf16[64,32,512]{2,0,1:T(8,128)(2,1)}), bf16[64,32,512]{2,0,1:T(8,128)(2,1)S(1)}, u32[]{:S(2)}, u32[]{:S(2)}) async-start(bf16[64,32,512]{2,0,1:T(8,128)(2,1)} %convert_bitcast_fusion.1), calls=%async_computation.1 | async-start | bytes 4194304 | tf_op jit(solution)/shard_map/all_to_all | solution.py:48
  85.2 151.6 %all-reduce.3.cloned.1.call-start = ((), (), s32[]{:S(2)}) async-start(), calls=%async_computation.6 | async-start | bytes 12582912 | tf_op jit(solution)/shard_map/psum | solution.py:52
  119.6 392.7 %all-reduce.5.cloned.1.call-start = ((), (), s32[]{:S(2)}) async-start(), calls=%async_computation.7 | async-start | bytes 12582912 | tf_op jit(solution)/shard_map/psum | solution.py:52
  297.9 2.1 copy-start
  300.3 44.1 %copy-start.2 = (f32[64,2048]{1,0:T(8,128)}, f32[64,2048]{1,0:T(8,128)S(1)}, u32[]{:S(2)}) copy-start(f32[64,2048]{1,0:T(8,128)S(1)} %get-tuple-element.12) | copy-start | bytes 1572868
  578.1 2.1 copy-start.3
  679.1 2.1 copy-start.1
Sparse Core Ops, SparseCore 0:
  119.7 117.0 all-reduce.2
  395.1 117.1 all-reduce.4
